TPU v7x, 512 devices: a whole 4x8x8 slice. The times are simulated.
512 devices in a mesh: space: 32 (over y_lo, z), chaos: 16 (over x, y_hi, core).
Axes of the slice: x: 4, y: 8 (y_hi: 2, y_lo: 4; y = y_hi * 4 + y_lo), z: 8, core: 2. Of those that a mesh axis runs over, the one named last changes fastest.
Arguments:
- load_vectors: bfloat16 [256, 2, 16, 12288], P('chaos', None, None, 'space'), may hold values from -6 to 6
- stiff_tiles: bfloat16 [128, 3, 8, 2, 96, 96], P('space'), may hold values from -0.09375 to 0.09375
- tile_columns: int32 [128, 3], P('space'), may hold values from 0 to 5, as said below
- chaos_index: int32 [8, 256, 32], replicated, may hold values from 0 to 255, as said below
- chaos_value: bfloat16 [8, 256, 32], replicated, may hold values from -1 to 1
Outputs:
- response: float32 [256, 2, 16, 12288], P('chaos', None, None, 'space')
Inputs may be any that keep to these rules, and one draw needn't show every extreme that they name: `tile_columns`: in row b of one subdomain with local index l = b % 4, the three numbers are l + 1, one of 0 to l, and one of l + 2 to 5. `chaos_index`: for every k and i the 32 numbers are distinct and the first is i.
All inputs are finite; a program needn't handle non-finite values.
Results may differ from a plain program's by a relative error of at most 0.0029.
Values may be sent and summed in bfloat16 or wider, within the bound.
A program may use at most 128 MiB of HBM per device.

v0:
```python
import jax
import jax.numpy as jnp
from jax import lax
from jax.sharding import PartitionSpec as P

TILE = 96
NKL = 8
P_SIZE = 256


def with_halo(cells, sides, width):
    for axis, dim in sides:
        count = lax.axis_size(axis)
        ends = count - 1
        head = lax.slice_in_dim(cells, 0, width, axis=dim)
        tail = lax.slice_in_dim(cells, cells.shape[dim] - width, cells.shape[dim], axis=dim)
        cells = jnp.concatenate(
            [
                lax.ppermute(tail, axis, [(i, (i + 1) % count) for i in range(ends)]),
                cells,
                lax.ppermute(head, axis, [((i + 1) % count, i) for i in range(ends)]),
            ],
            axis=dim,
        )
    return cells


def dense_coupling(chaos_index, chaos_value):
    columns = jnp.arange(P_SIZE, dtype=jnp.int32)

    def one_term(index_pair):
        row_index, row_value = index_pair
        matches = row_index[:, :, None] == columns[None, None, :]
        summed = jnp.where(matches, row_value[:, :, None], jnp.zeros((), jnp.bfloat16)).sum(axis=1)
        return summed

    return lax.map(one_term, (chaos_index, chaos_value))


def body(load_vectors, stiff_tiles, tile_columns, chaos_index, chaos_value):
    extended = with_halo(load_vectors, (("space", 3),), TILE)
    own_terms = load_vectors.shape[0]
    blocks = stiff_tiles.shape[0]
    first_term = lax.axis_index("chaos") * own_terms
    own_index = lax.dynamic_slice_in_dim(chaos_index, first_term, own_terms, 1)
    own_value = lax.dynamic_slice_in_dim(chaos_value, first_term, own_terms, 1)
    coupling = dense_coupling(own_index, own_value)
    coupled_field = jnp.einsum(
        "kij,jcre->kicre",
        coupling,
        lax.all_gather(extended, "chaos", axis=0, tiled=True),
        preferred_element_type=jnp.float32,
    ).astype(jnp.bfloat16)
    terms = coupled_field.shape[1]
    cases = coupled_field.shape[3]
    coupled_field = coupled_field.reshape(NKL, terms, 2, cases, blocks + 2, TILE)
    real_part = stiff_tiles[:, :, :, 0]
    imag_part = stiff_tiles[:, :, :, 1]
    upper_row = jnp.stack([real_part, -imag_part], axis=3)
    lower_row = jnp.stack([imag_part, real_part], axis=3)
    complex_tiles = jnp.stack([upper_row, lower_row], axis=3)
    accum_sum = jnp.zeros((terms, 2, cases, blocks, TILE), jnp.float32)
    for tile_slot in range(stiff_tiles.shape[1]):
        columns = jnp.take(coupled_field, tile_columns[:, tile_slot], axis=4)
        accum_sum = accum_sum + jnp.einsum(
            "bkcdxy,kidrby->icrbx",
            complex_tiles[:, tile_slot],
            columns,
            preferred_element_type=jnp.float32,
        )
    result = accum_sum.reshape(terms, 2, cases, blocks * TILE)
    return result


def solution(mesh):
    in_specs = (
        P("chaos", None, None, "space"),
        P("space", None, None, None, None, None),
        P("space", None),
        P(),
        P(),
    )
    out_specs = P("chaos", None, None, "space")
    return jax.shard_map(body, mesh=mesh, in_specs=in_specs, out_specs=out_specs, check_vma=False)
```

profile of v0, /device:TPU:9, one launch (start us, length us, event | category | flops | bytes accessed | tf_op | source)
XLA Modules:
  0.0 222.4 jit_solution(17434653015442165927)
XLA Ops:
  6.5 1.2 copy.32
  7.8 10.6 %collective-permute-start.1 = (bf16[16,2,16,96]{3,0,2,1:T(8,128)(2,1)S(1)}, bf16[16,2,16,96]{3,0,2,1:T(8,128)(2,1)S(1)}, u32[]{:S(2)}, u32[]{:S(2)}) collective-permute-start(bf16[16,2,16,96]{3,0,2,1:T(8,128)(2,1)S(1)} %get-tuple-element.96), channel_id=1, source_target_pairs={{16,0},{32,16},{48,32},{64,48},{80,64},{96,80},{112,96},{128,112},... | collective-permute-start | bytes 294920 | tf_op jit(solution)/shard_map/ppermute | solution.py:21
  18.4 1.9 collective-permute-start
  20.5 5.7 %collective-permute-done = bf16[16,2,16,96]{3,0,2,1:T(8,128)(2,1)S(1)} collective-permute-done((bf16[16,2,16,96]{3,0,2,1:T(8,128)(2,1)S(1)}, bf16[16,2,16,96]{3,0,2,1:T(8,128)(2,1)S(1)}, u32[]{:S(2)}, u32[]{:S(2)}) %collective-permute-start) | collective-permute-done | bytes 98336 | tf_op jit(solution)/shard_map/ppermute | solution.py:19
  26.2 1.2 pad_maximum_fusion.2
  27.6 0.9 constant_dynamic-slice_fusion
  28.7 1.0 slice_reduce_fusion
  29.8 3.3 %fusion.58 = (bf16[4,3,8,1,96,96]{5,4,3,2,1,0:T(8,128)(2,1)S(1)}, bf16[4,3,8,1,96,96]{5,4,3,2,1,0:T(8,128)(2,1)S(1)}) fusion(bf16[4,3,8,2,96,96]{5,4,3,2,1,0:T(8,128)(2,1)} %param.10), kind=kLoop, calls=%fused_computation.62 | loop fusion | bytes 7077888 | tf_op jit(solution)/shard_map/slice | solution.py:57
  33.0 0.3 copy_negate_fusion
  33.3 5.0 %maximum_bitcast_fusion = (bf16[4,3,8,1,2,96,96]{6,5,2,4,3,0,1:T(8,128)(2,1)}, bf16[4,3,8,1,2,96,96]{6,5,2,4,3,0,1:T(8,128)(2,1)}) fusion(bf16[4,3,8,1,96,96]{5,4,2,3,0,1:T(8,128)(2,1)S(1)} %copy_negate_fusion, bf16[4,3,8,1,96,96]{5,4,3,2,1,0:T(8,128)(2,1)S(1)} %get-tuple-element.93, bf16[4,3,8,1,96,96]{5,4,3,2,1,0:T(8,128)(2,1)S(1)} %get-tuple-element.94), kind=kLoop, calls=%fused_computation.16 | loop fusion | flops 8847360 | bytes 12386304 | tf_op jit(solution)/shard_map/stack | solution.py:61
  38.4 2.4 %while.13 = (s32[]{:T(128)}, bf16[8,16,256]{2,1,0:T(8,128)(2,1)S(1)}, s32[8,16,32]{2,1,0:T(8,128)S(1)}, bf16[8,16,32]{2,1,0:T(8,128)(2,1)S(1)}, s32[]{:T(128)}) while((s32[]{:T(128)}, bf16[8,16,256]{2,1,0:T(8,128)(2,1)S(1)}, s32[8,16,32]{2,1,0:T(8,128)S(1)}, bf16[8,16,32]{2,1,0:T(8,128)(2,1)S(1)}, s32[]{:T(128)}) %tuple.37), condition=%wide.region_2.3_spmd.clone, body=%wide.region_0.2_spmd.clone.sunk | while | flops 389122 | bytes 33873 | solution.py:37
  40.8 113.3 %all-gather.2.cloned.1.call-done = bf16[256,2,16,576]{3,0,2,1:T(8,128)(2,1)} async-done(((bf16[16,2,16,576]{3,0,2,1:T(8,128)(2,1)}), bf16[256,2,16,576]{3,0,2,1:T(8,128)(2,1)}) %all-gather.2.cloned.1.call-update) | async-done | bytes 9437200 | tf_op jit(solution)/shard_map/all_gather | solution.py:51
  154.0 7.9 %fusion.21 = bf16[8,16,2,16,576]{4,1,3,2,0:T(8,128)(2,1)} fusion(bf16[256,2,16,576]{3,0,2,1:T(8,128)(2,1)} %all-gather.2.cloned.1.call-done, bf16[8,16,256]{2,1,0:T(8,128)(2,1)S(1)} %get-tuple-element.71), kind=kOutput, calls=%fused_computation.35 | convolution fusion | flops 1210318848 | bytes 14221312 | tf_op jit(solution)/shard_map/kij,jcre->kicre/dot_general | solution.py:48
  161.9 13.6 %reshape.62 = bf16[8,16,2,16,6,96]{5,4,1,3,2,0:T(8,128)(2,1)} reshape(bf16[8,16,2,16,576]{4,1,3,2,0:T(8,128)(2,1)} %fusion.21) | data formatting | bytes 9437184 | tf_op jit(solution)/shard_map/reshape | solution.py:56
  175.5 10.1 %copy.36 = bf16[8,16,2,16,6,96]{5,3,2,1,0,4:T(8,128)(2,1)} copy(bf16[8,16,2,16,6,96]{5,4,1,3,2,0:T(8,128)(2,1)} %reshape.62) | data formatting | bytes 9437184 | tf_op jit(solution)/shard_map/reshape | solution.py:56
  185.7 5.8 %gather_fusion = bf16[4,8,16,2,16,96]{5,4,3,2,1,0:T(8,128)(2,1)} fusion(bf16[8,16,2,16,6,96]{5,3,2,1,0,4:T(8,128)(2,1)} %copy.36, s32[1024]{0:T(1024)S(1)} %pad_clamp_fusion.2), kind=kCustom, calls=%fused_computation.clone | custom fusion | bytes 6291472 | tf_op jit(solution)/shard_map/jit(_take)/gather | solution.py:64
  191.5 5.8 %gather_fusion.1 = bf16[4,8,16,2,16,96]{5,4,3,2,1,0:T(8,128)(2,1)} fusion(bf16[8,16,2,16,6,96]{5,3,2,1,0,4:T(8,128)(2,1)} %copy.36, s32[1024]{0:T(1024)S(1)} %pad_clamp_fusion.1), kind=kCustom, calls=%fused_computation.1.clone | custom fusion | bytes 6291472 | tf_op jit(solution)/shard_map/jit(_take)/gather | solution.py:64
  197.3 5.9 %gather_fusion.2 = bf16[4,8,16,2,16,96]{5,4,3,2,1,0:T(8,128)(2,1)} fusion(bf16[8,16,2,16,6,96]{5,3,2,1,0,4:T(8,128)(2,1)} %copy.36, s32[1024]{0:T(1024)S(1)} %pad_clamp_fusion), kind=kCustom, calls=%fused_computation.2.clone | custom fusion | bytes 6291472 | tf_op jit(solution)/shard_map/jit(_take)/gather | solution.py:64
  203.2 4.6 %fusion.24 = f32[4,16,16,2,96]{4,2,3,1,0:T(8,128)S(1)} fusion(bf16[4,3,8,1,2,96,96]{6,5,2,4,3,0,1:T(8,128)(2,1)} %get-tuple-element.101, bf16[4,3,8,1,2,96,96]{6,5,2,4,3,0,1:T(8,128)(2,1)} %get-tuple-element.102, bf16[4,8,16,2,16,96]{5,4,3,2,1,0:T(8,128)(2,1)} %gather_fusion, pred[4]{0:T(512)(128)(4,1)S(1)} %compare_and_fusion.2), kind=kOutput, calls=%fused_computation.37 | convolution fusion | flops 610271232 | bytes 11010052 | tf_op jit(solution)/shard_map/bkcdxy,kidrby->icrbx/dot_general | solution.py:65
  207.8 1.0 copy-done.3
  208.8 3.1 %fusion.49 = f32[4,16,16,2,96]{4,2,3,1,0:T(8,128)S(1)} fusion(f32[4,16,16,2,96]{4,2,3,1,0:T(8,128)S(1)} %fusion.24, bf16[4,3,8,1,2,96,96]{6,5,2,4,3,0,1:T(8,128)(2,1)S(1)} %bitcast.101, bf16[4,3,8,1,2,96,96]{6,5,2,4,3,0,1:T(8,128)(2,1)} %get-tuple-element.102, bf16[4,8,16,2,16,96]{5,4,3,2,1,0:T(8,128)(2,1)S(1)} %copy-done.3, ...), kind=kOutput, calls=%fused_computation.42 | convolution fusion | flops 610467840 | bytes 11796484 | tf_op jit(solution)/shard_map/bkcdxy,kidrby->icrbx/dot_general | solution.py:65
  212.1 1.4 fusion.44
  213.4 0.7 copy.45
  214.2 1.4 reshape.17
  (64 shorter events, 2.9 us)
Async XLA Ops:
  6.5 20.9 %copy-start = (s32[8,256,32]{1,2,0:T(8,128)S(1)}, s32[8,256,32]{1,2,0:T(8,128)}, u32[]{:S(2)}) copy-start(s32[8,256,32]{1,2,0:T(8,128)} %param.12) | copy-start | bytes 786436
  6.5 147.5 %all-gather.2.cloned.1.call-start = ((), (), s32[]{:S(2)}) async-start(), calls=%async_computation | async-start | bytes 11141120 | tf_op jit(solution)/shard_map/all_gather | solution.py:51
  7.8 12.7 %collective-permute-start.1 = (bf16[16,2,16,96]{3,0,2,1:T(8,128)(2,1)S(1)}, bf16[16,2,16,96]{3,0,2,1:T(8,128)(2,1)S(1)}, u32[]{:S(2)}, u32[]{:S(2)}) collective-permute-start(bf16[16,2,16,96]{3,0,2,1:T(8,128)(2,1)S(1)} %get-tuple-element.96), channel_id=1, source_target_pairs={{16,0},{32,16},{48,32},{64,48},{80,64},{96,80},{112,96},{128,112},... | collective-permute-start | bytes 294920 | tf_op jit(solution)/shard_map/ppermute | solution.py:21
  18.4 7.8 %collective-permute-start = (bf16[16,2,16,96]{3,0,2,1:T(8,128)(2,1)S(1)}, bf16[16,2,16,96]{3,0,2,1:T(8,128)(2,1)S(1)}, u32[]{:S(2)}, u32[]{:S(2)}) collective-permute-start(bf16[16,2,16,96]{3,0,2,1:T(8,128)(2,1)S(1)} %get-tuple-element.95), channel_id=1, source_target_pairs={{0,16},{16,32},{32,48},{48,64},{64,80},{80,96},{96,112},{112,128},... | collective-permute-start | bytes 294920 | tf_op jit(solution)/shard_map/ppermute | solution.py:19
  197.3 10.5 %slice-start = ((s8[4718592]{0:T(1024)(128)(4,1)}), s8[524288]{0:T(1024)(128)(4,1)S(1)}, s32[]{:S(2)}) async-start(s8[4718592]{0:T(1024)(128)(4,1)} %bitcast.100), calls=%async_computation.1 | async-start | bytes 1048576
  203.2 4.6 %slice-start.1 = ((s8[4718592]{0:T(1024)(128)(4,1)}), s8[4194304]{0:T(1024)(128)(4,1)S(1)}, s32[]{:S(2)}) async-start(s8[4718592]{0:T(1024)(128)(4,1)} %bitcast.100), calls=%async_computation.2 | async-start | bytes 8388608
  203.2 5.6 %copy-start.3 = (bf16[4,8,16,2,16,96]{5,4,3,2,1,0:T(8,128)(2,1)S(1)}, bf16[4,8,16,2,16,96]{5,4,3,2,1,0:T(8,128)(2,1)}, u32[]{:S(2)}) copy-start(bf16[4,8,16,2,16,96]{5,4,3,2,1,0:T(8,128)(2,1)} %gather_fusion.1) | copy-start | bytes 9437188
  203.2 8.8 %slice-start.2 = ((s8[4718592]{0:T(1024)(128)(4,1)}), s8[4194304]{0:T(1024)(128)(4,1)S(1)}, s32[]{:S(2)}) async-start(s8[4718592]{0:T(1024)(128)(4,1)} %bitcast.102), calls=%async_computation.3 | async-start | bytes 8388608
  208.8 3.1 %slice-start.3 = ((s8[4718592]{0:T(1024)(128)(4,1)}), s8[524288]{0:T(1024)(128)(4,1)S(1)}, s32[]{:S(2)}) async-start(s8[4718592]{0:T(1024)(128)(4,1)} %bitcast.102), calls=%async_computation.4 | async-start | bytes 1048576
  208.8 3.2 %copy-start.2 = (bf16[4,8,16,2,16,96]{5,4,3,2,1,0:T(8,128)(2,1)S(1)}, bf16[4,8,16,2,16,96]{5,4,3,2,1,0:T(8,128)(2,1)}, u32[]{:S(2)}) copy-start(bf16[4,8,16,2,16,96]{5,4,3,2,1,0:T(8,128)(2,1)} %gather_fusion.2) | copy-start | bytes 9437188
  212.1 3.5 %copy-start.1 = (s32[8,256,32]{1,2,0:T(8,128)S(1)}, s32[8,256,32]{1,2,0:T(8,128)}, u32[]{:S(2)}) copy-start(s32[8,256,32]{1,2,0:T(8,128)} %param.12) | copy-start | bytes 786436
Sparse Core Ops, SparseCore 0:
  27.5 126.4 all-gather.1
where the time goes:
time: 223 us; the launch traced here: 222 us
  waiting for transfers between devices  119 us (53%)
  local copies, waits for them, and re-layouts  51.5 us (23%)
  matrix products  16.9 us (8%)
  between operations  13.6 us (6%)
  starting transfers between devices  12.5 us (6%)
  other arithmetic  8.46 us (4%)
    all_gather x1, waiting for transfers between devices, body(): lax.all_gather(extended, 'chaos', axis=0, tiled=True)  113 us
    reshape x2, local copies, waits for them, and re-layouts, body(): coupled_field.reshape(NKL, terms, 2, cases, blocks + 2, TILE)  23.7 us
    gather x3, local copies, waits for them, and re-layouts, body(): columns = jnp.take(coupled_field, tile_columns[:, tile_slot], axis=4)  17.5 us
    ppermute x1, starting transfers between devices, with_halo(): lax.ppermute(head, axis, [((i + 1) % count, i) for i in range(ends)])  10.6 us
    dot_general x3, matrix products, body(): jnp.einsum('bkcdxy,kidrby->icrbx', complex_tiles[:, tile_slot], columns,...  9.03 us
    dot_general x1, matrix products, body(): jnp.einsum('kij,jcre->kicre', coupling, lax.all_gather(extended, 'chaos',...  7.9 us
    ppermute x1, waiting for transfers between devices, with_halo(): lax.ppermute(tail, axis, [(i, (i + 1) % count) for i in range(ends)])  5.66 us
    another operation x1, other arithmetic, body(): complex_tiles = jnp.stack([upper_row, lower_row], axis=3)  5.02 us
  transfers between devices with their start and end apart: 3, of which 3 were waited for; matrix products, arithmetic and copies ran while one was open for 6% of the time, Pallas kernels for 0%

commit v1 on v0

--- a/solution.py
+++ b/solution.py
@@ -48,7 +48,9 @@
     coupled_field = jnp.einsum(
         "kij,jcre->kicre",
         coupling,
-        lax.all_gather(extended, "chaos", axis=0, tiled=True),
+        jnp.concatenate(
+            lax.all_to_all(jnp.stack([extended] * lax.axis_size("chaos")), "chaos", 0, 0), axis=0
+        ),
         preferred_element_type=jnp.float32,
     ).astype(jnp.bfloat16)
     terms = coupled_field.shape[1]

time: 223 us -> 349 us (1.57)
  the two profiles are of different devices: /device:TPU:9 before, /device:TPU:214 now
where the time goes in v1:
time: 349 us; the launch traced here: 348 us
  waiting for transfers between devices  235 us (67%)
  local copies, waits for them, and re-layouts  70.5 us (20%)
  matrix products  18.1 us (5%)
  starting transfers between devices  15.8 us (5%)
  other arithmetic  8.61 us (2%)
    all_to_all x1, waiting for transfers between devices, body(): lax.all_to_all(jnp.stack([extended] * lax.axis_size('chaos')), 'chaos', 0...  229 us
    reshape x2, local copies, waits for them, and re-layouts, body(): coupled_field.reshape(NKL, terms, 2, cases, blocks + 2, TILE)  23.6 us
    gather x3, local copies, waits for them, and re-layouts, body(): columns = jnp.take(coupled_field, tile_columns[:, tile_slot], axis=4)  17.8 us
    reshape x1, local copies, waits for them, and re-layouts, body(): jnp.concatenate(lax.all_to_all(jnp.stack([extended] * lax.axis_size('chao...  15.3 us
    dot_general x1, matrix products, body(): jnp.einsum('kij,jcre->kicre', coupling, jnp.concatenate(lax.all_to_all(jn...  9.27 us
    dot_general x3, matrix products, body(): jnp.einsum('bkcdxy,kidrby->icrbx', complex_tiles[:, tile_slot], columns,...  8.81 us
    all_to_all x1, starting transfers between devices, body(): lax.all_to_all(jnp.stack([extended] * lax.axis_size('chaos')), 'chaos', 0...  8.39 us
  transfers between devices with their start and end apart: 3, of which 3 were waited for; matrix products, arithmetic and copies ran while one was open for 3% of the time, Pallas kernels for 0%

profile of v1, /device:TPU:214, one launch (start us, length us, event | category | flops | bytes accessed | tf_op | source)
XLA Modules:
  0.0 348.3 jit_solution(10360924640731632063)
XLA Ops:
  0.0 1.1 fusion.59
  1.1 5.5 %collective-permute-start = (bf16[16,2,16,96]{3,2,1,0:T(8,128)(2,1)S(1)}, bf16[16,2,16,96]{3,2,1,0:T(8,128)(2,1)S(1)}, u32[]{:S(2)}, u32[]{:S(2)}) collective-permute-start(bf16[16,2,16,96]{3,2,1,0:T(8,128)(2,1)S(1)} %get-tuple-element.95), channel_id=1, source_target_pairs={{0,16},{16,32},{32,48},{48,64},{64,80},{80,96},{96,112},{112,128},... | collective-permute-start | bytes 294920 | tf_op jit(solution)/shard_map/ppermute | solution.py:19
  6.6 1.9 collective-permute-start.1
  8.5 0.8 collective-permute-done
  9.4 5.3 %collective-permute-done.1 = bf16[16,2,16,96]{3,2,1,0:T(8,128)(2,1)S(1)} collective-permute-done((bf16[16,2,16,96]{3,2,1,0:T(8,128)(2,1)S(1)}, bf16[16,2,16,96]{3,2,1,0:T(8,128)(2,1)S(1)}, u32[]{:S(2)}, u32[]{:S(2)}) %collective-permute-start.1) | collective-permute-done | bytes 98336 | tf_op jit(solution)/shard_map/ppermute | solution.py:21
  14.7 1.4 pad_maximum_fusion.2
  16.0 5.2 %stack.12 = bf16[16,16,2,16,576]{4,3,2,1,0:T(8,128)(2,1)} broadcast(bf16[16,2,16,576]{3,2,1,0:T(8,128)(2,1)S(1)} %pad_maximum_fusion.2), dimensions={1,2,3,4} | broadcast | bytes 10027008 | tf_op jit(solution)/shard_map/stack | solution.py:52
  21.2 8.4 %all-to-all-start = ((bf16[16,16,2,16,576]{4,3,2,1,0:T(8,128)(2,1)}), bf16[16,16,2,16,576]{4,3,2,1,0:T(8,128)(2,1)}, u32[]{:S(2)}, u32[]{:S(2)}) async-start(bf16[16,16,2,16,576]{4,3,2,1,0:T(8,128)(2,1)} %stack.12), calls=%async_computation | async-start | bytes 20971520 | tf_op jit(solution)/shard_map/all_to_all | solution.py:52
  30.4 3.3 fusion.58
  34.0 5.0 %maximum_bitcast_fusion = (bf16[4,3,8,1,2,96,96]{6,5,2,4,3,0,1:T(8,128)(2,1)}, bf16[4,3,8,1,2,96,96]{6,5,2,4,3,0,1:T(8,128)(2,1)}) fusion(bf16[4,3,8,1,96,96]{5,4,2,3,0,1:T(8,128)(2,1)S(1)} %copy_negate_fusion, bf16[4,3,8,1,96,96]{5,4,3,2,1,0:T(8,128)(2,1)S(1)} %get-tuple-element.93, bf16[4,3,8,1,96,96]{5,4,3,2,1,0:T(8,128)(2,1)S(1)} %get-tuple-element.94), kind=kLoop, calls=%fused_computation.16 | loop fusion | flops 8847360 | bytes 12386304 | tf_op jit(solution)/shard_map/stack | solution.py:63
  38.9 2.4 while.13
  41.4 228.6 %all-to-all-done = bf16[16,16,2,16,576]{4,3,2,1,0:T(8,128)(2,1)} async-done(((bf16[16,16,2,16,576]{4,3,2,1,0:T(8,128)(2,1)}), bf16[16,16,2,16,576]{4,3,2,1,0:T(8,128)(2,1)}, u32[]{:S(2)}, u32[]{:S(2)}) %all-to-all-start) | async-done | bytes 9437216 | tf_op jit(solution)/shard_map/all_to_all | solution.py:52
  270.0 15.3 %copy.28 = bf16[256,2,16,576]{0,3,2,1:T(8,128)(2,1)} copy(bf16[256,2,16,576]{3,2,1,0:T(8,128)(2,1)} %bitcast.2) | data formatting | bytes 18874368 | tf_op jit(solution)/shard_map/reshape | solution.py:51
  285.3 9.3 %fusion.21 = bf16[8,16,2,16,576]{4,1,3,2,0:T(8,128)(2,1)} fusion(bf16[256,2,16,576]{0,3,2,1:T(8,128)(2,1)} %copy.28, bf16[8,16,256]{2,1,0:T(8,128)(2,1)S(1)} %get-tuple-element.71), kind=kOutput, calls=%fused_computation.35 | convolution fusion | flops 1210318848 | bytes 14221312 | tf_op jit(solution)/shard_map/kij,jcre->kicre/dot_general | solution.py:48
  294.6 13.6 %reshape.68 = bf16[8,16,2,16,6,96]{5,4,1,3,2,0:T(8,128)(2,1)} reshape(bf16[8,16,2,16,576]{4,1,3,2,0:T(8,128)(2,1)} %fusion.21) | data formatting | bytes 9437184 | tf_op jit(solution)/shard_map/reshape | solution.py:58
  308.2 10.0 %copy.30 = bf16[8,16,2,16,6,96]{5,3,2,1,0,4:T(8,128)(2,1)} copy(bf16[8,16,2,16,6,96]{5,4,1,3,2,0:T(8,128)(2,1)} %reshape.68) | data formatting | bytes 9437184 | tf_op jit(solution)/shard_map/reshape | solution.py:58
  318.2 5.9 %gather_fusion = bf16[4,8,16,2,16,96]{5,4,3,2,1,0:T(8,128)(2,1)} fusion(bf16[8,16,2,16,6,96]{5,3,2,1,0,4:T(8,128)(2,1)} %copy.30, s32[1024]{0:T(1024)S(1)} %pad_clamp_fusion.2), kind=kCustom, calls=%fused_computation.clone | custom fusion | bytes 6291472 | tf_op jit(solution)/shard_map/jit(_take)/gather | solution.py:66
  324.1 5.9 %gather_fusion.1 = bf16[4,8,16,2,16,96]{5,4,3,2,1,0:T(8,128)(2,1)} fusion(bf16[8,16,2,16,6,96]{5,3,2,1,0,4:T(8,128)(2,1)} %copy.30, s32[1024]{0:T(1024)S(1)} %pad_clamp_fusion.1), kind=kCustom, calls=%fused_computation.1.clone | custom fusion | bytes 6291472 | tf_op jit(solution)/shard_map/jit(_take)/gather | solution.py:66
  329.9 6.0 %gather_fusion.2 = bf16[4,8,16,2,16,96]{5,4,3,2,1,0:T(8,128)(2,1)} fusion(bf16[8,16,2,16,6,96]{5,3,2,1,0,4:T(8,128)(2,1)} %copy.30, s32[1024]{0:T(1024)S(1)} %pad_clamp_fusion), kind=kCustom, calls=%fused_computation.2.clone | custom fusion | bytes 6291472 | tf_op jit(solution)/shard_map/jit(_take)/gather | solution.py:66
  336.0 4.6 %fusion.24 = f32[4,16,16,2,96]{4,2,3,1,0:T(8,128)S(1)} fusion(bf16[4,3,8,1,2,96,96]{6,5,2,4,3,0,1:T(8,128)(2,1)} %get-tuple-element.101, bf16[4,3,8,1,2,96,96]{6,5,2,4,3,0,1:T(8,128)(2,1)} %get-tuple-element.102, bf16[4,8,16,2,16,96]{5,4,3,2,1,0:T(8,128)(2,1)} %gather_fusion, pred[4]{0:T(512)(128)(4,1)S(1)} %compare_and_fusion.2), kind=kOutput, calls=%fused_computation.37 | convolution fusion | flops 610271232 | bytes 11010052 | tf_op jit(solution)/shard_map/bkcdxy,kidrby->icrbx/dot_general | solution.py:67
  340.6 1.0 copy-done.3
  341.6 2.9 fusion.49
  344.9 1.4 fusion.44
  346.9 1.4 reshape.23
  (68 shorter events, 4.1 us)
Async XLA Ops:
  0.0 29.6 %copy-start = (s32[8,256,32]{1,2,0:T(8,128)S(1)}, s32[8,256,32]{1,2,0:T(8,128)}, u32[]{:S(2)}) copy-start(s32[8,256,32]{1,2,0:T(8,128)} %param.12) | copy-start | bytes 786436
  1.1 8.2 %collective-permute-start = (bf16[16,2,16,96]{3,2,1,0:T(8,128)(2,1)S(1)}, bf16[16,2,16,96]{3,2,1,0:T(8,128)(2,1)S(1)}, u32[]{:S(2)}, u32[]{:S(2)}) collective-permute-start(bf16[16,2,16,96]{3,2,1,0:T(8,128)(2,1)S(1)} %get-tuple-element.95), channel_id=1, source_target_pairs={{0,16},{16,32},{32,48},{48,64},{64,80},{80,96},{96,112},{112,128},... | collective-permute-start | bytes 294920 | tf_op jit(solution)/shard_map/ppermute | solution.py:19
  6.6 8.1 %collective-permute-start.1 = (bf16[16,2,16,96]{3,2,1,0:T(8,128)(2,1)S(1)}, bf16[16,2,16,96]{3,2,1,0:T(8,128)(2,1)S(1)}, u32[]{:S(2)}, u32[]{:S(2)}) collective-permute-start(bf16[16,2,16,96]{3,2,1,0:T(8,128)(2,1)S(1)} %get-tuple-element.96), channel_id=1, source_target_pairs={{16,0},{32,16},{48,32},{64,48},{80,64},{96,80},{112,96},{128,112},... | collective-permute-start | bytes 294920 | tf_op jit(solution)/shard_map/ppermute | solution.py:21
  21.2 8.6 %copy-start.4 = (bf16[8,256,32]{1,2,0:T(8,128)(2,1)S(1)}, bf16[8,256,32]{1,2,0:T(8,128)(2,1)}, u32[]{:S(2)}) copy-start(bf16[8,256,32]{1,2,0:T(8,128)(2,1)} %param.13) | copy-start | bytes 393220
  21.2 8.8 %copy-start.5 = (s32[4,3]{1,0:T(4,128)S(1)}, s32[4,3]{1,0:T(4,128)}, u32[]{:S(2)}) copy-start(s32[4,3]{1,0:T(4,128)} %param.11) | copy-start | bytes 148
  21.2 248.7 %all-to-all-start = ((bf16[16,16,2,16,576]{4,3,2,1,0:T(8,128)(2,1)}), bf16[16,16,2,16,576]{4,3,2,1,0:T(8,128)(2,1)}, u32[]{:S(2)}, u32[]{:S(2)}) async-start(bf16[16,16,2,16,576]{4,3,2,1,0:T(8,128)(2,1)} %stack.12), calls=%async_computation | async-start | bytes 20971520 | tf_op jit(solution)/shard_map/all_to_all | solution.py:52
  329.9 10.6 %slice-start = ((s8[4718592]{0:T(1024)(128)(4,1)}), s8[524288]{0:T(1024)(128)(4,1)S(1)}, s32[]{:S(2)}) async-start(s8[4718592]{0:T(1024)(128)(4,1)} %bitcast.101), calls=%async_computation.1 | async-start | bytes 1048576
  336.0 4.6 %slice-start.1 = ((s8[4718592]{0:T(1024)(128)(4,1)}), s8[4194304]{0:T(1024)(128)(4,1)S(1)}, s32[]{:S(2)}) async-start(s8[4718592]{0:T(1024)(128)(4,1)} %bitcast.101), calls=%async_computation.2 | async-start | bytes 8388608
  336.0 5.6 %copy-start.3 = (bf16[4,8,16,2,16,96]{5,4,3,2,1,0:T(8,128)(2,1)S(1)}, bf16[4,8,16,2,16,96]{5,4,3,2,1,0:T(8,128)(2,1)}, u32[]{:S(2)}) copy-start(bf16[4,8,16,2,16,96]{5,4,3,2,1,0:T(8,128)(2,1)} %gather_fusion.1) | copy-start | bytes 9437188
  336.0 8.5 %slice-start.2 = ((s8[4718592]{0:T(1024)(128)(4,1)}), s8[4194304]{0:T(1024)(128)(4,1)S(1)}, s32[]{:S(2)}) async-start(s8[4718592]{0:T(1024)(128)(4,1)} %bitcast.103), calls=%async_computation.3 | async-start | bytes 8388608
  341.6 2.9 slice-start.3
  341.6 3.2 copy-start.2
  344.8 3.5 copy-start.1
